TPU v7x, 32 devices: a whole 2x2x4 slice. The times are simulated.
32 devices in a mesh: grp: 2 (over core), aux: 8 (over z, x), tr: 2 (over y).
Axes of the slice: x: 2, y: 2, z: 4, core: 2. Of those that a mesh axis runs over, the one named last changes fastest.
Arguments:
- trial_vectors: float32 [64, 8, 512], P('aux', None, 'tr'), may hold values from -6 to 6
- energy_val: float32 [64], P('aux'), may hold values from -1 to -0.2
- energy_cond: float32 [512], P('tr'), may hold values from 0.2 to 2
- coef_occ: bfloat16 [512, 64, 64], P('aux'), may hold values from -0.75 to 0.75
- coef_virt: bfloat16 [512, 512, 512], P('aux', 'tr'), may hold values from -0.01171875 to 0.01171875
- pair_coef: bfloat16 [64, 512, 512], P('aux', 'tr'), may hold values from -0.03125 to 0.03125
- live_aux: int32 [8], P('aux'), may hold values from 16 to 64, as said below
Outputs:
- applied: float32 [64, 8, 512], P('aux', None, 'tr')
- intersection: float32 [8, 8], replicated
Inputs may be any that keep to these rules, and one draw needn't show every extreme that they name: `live_aux`: equals 64 on at least one shard.
All inputs are finite; a program needn't handle non-finite values.
Results may differ from a plain program's by a relative error of at most 0.0048.
Values may be sent and summed in bfloat16 or wider, within the bound.
A program may use at most 64 MiB of HBM per device.

v0:
```python
import math

import jax
import jax.numpy as jnp
from jax import lax
from jax.sharding import PartitionSpec as P

V = 64
C = 512


def apply_hamiltonian(vectors, energy_gap, coef_occ, coef_virt, pair_coef, live_aux):
    rounded = vectors.astype(jnp.bfloat16)
    gathered = lax.all_gather(rounded, "aux", axis=0, tiled=True)
    group_index = lax.axis_index("grp")
    slots = coef_occ.shape[0]
    live_count = live_aux[0]
    zero_slot = jnp.zeros((), jnp.int32)
    range_high = jnp.where(group_index == 0, live_count, zero_slot)
    block_size = math.gcd(slots, 8)
    first_block = zero_slot // block_size
    last_block = (range_high + block_size - 1) // block_size
    full_vectors = gathered.shape[1]
    full_cond = coef_virt.shape[2]

    def one_block(block_index, running):
        slot_start = block_index * block_size
        piece_occ = lax.dynamic_slice_in_dim(coef_occ, slot_start, block_size, 0)
        piece_virt = lax.dynamic_slice_in_dim(coef_virt, slot_start, block_size, 0)
        slot_ids = slot_start + lax.iota(jnp.int32, block_size)
        keep_mask = ((slot_ids >= zero_slot) & (slot_ids < range_high)).astype(jnp.float32)
        blended = jnp.einsum(
            "puv,vkc->pukc", piece_occ, gathered, preferred_element_type=jnp.float32
        )
        blended = (blended * keep_mask[:, None, None, None]).astype(jnp.bfloat16)
        return running + jnp.einsum(
            "pukc,pcd->ukd", blended, piece_virt, preferred_element_type=jnp.float32
        )

    zero_term = jnp.zeros((gathered.shape[0], full_vectors, full_cond), jnp.float32)
    direct_term = lax.fori_loop(first_block, last_block, one_block, zero_term)
    direct_term = lax.psum_scatter(direct_term, "tr", scatter_dimension=2, tiled=True)
    direct_term = lax.psum_scatter(direct_term, "aux", scatter_dimension=0, tiled=True)
    is_exchange = group_index == 1
    projection = lax.cond(
        is_exchange,
        lambda: jnp.einsum("vcp,vkc->kp", pair_coef, rounded, preferred_element_type=jnp.float32),
        lambda: jnp.zeros((vectors.shape[1], pair_coef.shape[2]), jnp.float32),
    )
    projection = lax.psum(projection, ("aux", "tr"))
    projection_b = projection.astype(jnp.bfloat16)
    exchange_term = lax.cond(
        is_exchange,
        lambda: jnp.einsum(
            "vcp,kp->vkc", pair_coef, projection_b, preferred_element_type=jnp.float32
        ),
        lambda: jnp.zeros(vectors.shape, jnp.float32),
    )
    combined = lax.psum(direct_term + exchange_term, "grp")
    return energy_gap[:, None, :] * vectors + combined


def body(trial_vectors, energy_val, energy_cond, coef_occ, coef_virt, pair_coef, live_aux):
    energy_gap = energy_cond[None, :] - energy_val[:, None]
    applied_first = apply_hamiltonian(
        trial_vectors, energy_gap, coef_occ, coef_virt, pair_coef, live_aux
    )
    partial_intersection = jnp.einsum(
        "vkc,vjc->kj", trial_vectors, applied_first, precision=lax.Precision.HIGHEST
    )
    intersection = lax.psum(partial_intersection, ("aux", "tr")) / (V * C)
    residual = applied_first - jnp.einsum(
        "vkc,kj->vjc", trial_vectors, intersection, precision=lax.Precision.HIGHEST
    )
    correction = residual / energy_gap[:, None, :]
    applied = apply_hamiltonian(correction, energy_gap, coef_occ, coef_virt, pair_coef, live_aux)
    return (applied, intersection)


def solution(mesh):
    in_specs = (
        P("aux", None, "tr"),
        P("aux"),
        P("tr"),
        P("aux", None, None),
        P("aux", "tr", None),
        P("aux", "tr", None),
        P("aux"),
    )
    out_specs = (P("aux", None, "tr"), P())
    return jax.shard_map(body, mesh=mesh, in_specs=in_specs, out_specs=out_specs, check_vma=False)
```

profile of v0, /device:TPU:0, one launch (start us, length us, event | category | flops | bytes accessed | tf_op | source)
XLA Modules:
  0.0 438.5 jit_solution(5328799634057705139)
XLA Ops:
  7.2 0.0 reduce-scatter.5.cloned.1.call-start
  7.9 0.8 convert_element_type.40
  8.7 32.5 %all_gather.6 = bf16[64,8,256]{2,1,0:T(8,128)(2,1)S(1)} all-gather(bf16[8,8,256]{2,1,0:T(8,128)(2,1)S(1)} %convert_element_type.40), channel_id=1, replica_groups=mesh['grp'=2,'aux'=8,'tr'=2] {'aux'}, dimensions={0}, use_global_device_ids=true | all-gather | bytes 294912 | tf_op jit(solution)/shard_map/all_gather | solution.py:14
  41.3 0.1 broadcast.62.clone
  41.4 0.0 copy-start
  41.4 23.4 %while.20 = (s32[]{:T(128)}, f32[64,8,512]{2,1,0:T(8,128)S(1)}, s32[]{:T(128)}, bf16[64,64,64]{2,1,0:T(8,128)(2,1)}, bf16[64,8,256]{2,1,0:T(8,128)(2,1)S(1)}, /*...) while((s32[]{:T(128)}, f32[64,8,512]{2,1,0:T(8,128)S(1)}, ...), condition=%wide.region_1.2_spmd, body=%wide.region_0.1_spmd.sunk | while | flops 1210318848 | bytes 12976363 | solution.py:41
  41.4 1.7 fusion.77
  43.2 4.2 fusion.78
  47.4 1.6 fusion.77
  49.0 4.2 fusion.78
  53.2 1.6 fusion.77
  54.8 4.2 fusion.78
  59.0 1.6 fusion.77
  60.7 4.2 fusion.78
  64.9 0.0 copy-start.2
  64.9 1.0 copy-done.2
  65.8 0.0 reduce-scatter.5.cloned.1.call-update
  65.8 0.0 reduce-scatter.7.cloned.1.call-start
  65.9 42.1 %reduce-scatter.5.cloned.1.call-done = f32[64,8,256]{2,1,0:T(8,128)} async-done(((f32[64,8,512]{2,1,0:T(8,128)}), f32[64,8,256]{2,1,0:T(8,128)}) %reduce-scatter.5.cloned.1.call-update) | async-done | bytes 524304 | tf_op jit(solution)/shard_map/reduce_scatter | solution.py:42
  108.0 0.0 reduce-scatter.7.cloned.1.call-update
  108.0 0.0 all-reduce.3.cloned.1.call-start
  108.0 0.0 copy-done
  108.1 0.0 copy-start.4
  108.1 0.0 copy-start.5
  108.1 0.0 copy-start.3
  108.1 75.9 %psum.35 = bf16[8,512]{1,0:T(8,128)(2,1)S(1)} all-reduce(f32[8,512]{1,0:T(8,128)S(1)} %get-tuple-element.306), channel_id=1, replica_groups=mesh['grp'=2,'aux'=8,'tr'=2] {'aux','tr'}, use_global_device_ids=true, to_apply=%region_6.7 | all-reduce | flops 4096 | bytes 24576 | tf_op jit(solution)/shard_map/psum | solution.py:50
  184.0 0.0 reduce-scatter.7.cloned.1.call-done
  184.0 1.5 add.77
  185.5 0.0 all-reduce.3.cloned.1.call-update
  185.5 0.0 reduce-scatter.9.cloned.1.call-start
  185.6 0.0 copy-done.4
  185.6 0.0 copy-done.5
  185.6 0.1 broadcast_subtract_fusion
  185.6 13.6 %all-reduce.3.cloned.1.call-done = f32[8,8,256]{2,1,0:T(8,128)} async-done(((f32[8,8,256]{2,1,0:T(8,128)}), f32[8,8,256]{2,1,0:T(8,128)}) %all-reduce.3.cloned.1.call-update) | async-done | bytes 65552 | tf_op jit(solution)/shard_map/psum | solution.py:59
  199.2 0.0 copy-done.3
  199.3 1.0 convolution_bitcast_fusion.5
  200.3 42.1 %psum.37 = f32[8,8]{0,1:T(8,128)S(1)} all-reduce(f32[8,8]{0,1:T(8,128)S(1)} %convolution_bitcast_fusion.5), channel_id=1, replica_groups=mesh['grp'=2,'aux'=8,'tr'=2] {'aux','tr'}, use_global_device_ids=true, to_apply=%region_10.11 | all-reduce | flops 64 | bytes 512 | tf_op jit(solution)/shard_map/psum | solution.py:71
  242.4 1.0 fusion.52
  243.5 30.8 %all_gather.7 = bf16[64,8,256]{2,1,0:T(8,128)(2,1)S(1)} all-gather(bf16[8,8,256]{2,1,0:T(8,128)(2,1)S(1)} %get-tuple-element.150), channel_id=1, replica_groups=mesh['grp'=2,'aux'=8,'tr'=2] {'aux'}, dimensions={0}, use_global_device_ids=true | all-gather | bytes 294912 | tf_op jit(solution)/shard_map/all_gather | solution.py:14
  274.2 0.1 broadcast.62
  274.4 23.3 %while.21 = (s32[]{:T(128)}, f32[64,8,512]{2,1,0:T(8,128)S(1)}, s32[]{:T(128)}, bf16[64,64,64]{2,1,0:T(8,128)(2,1)}, bf16[64,8,256]{2,1,0:T(8,128)(2,1)S(1)}, /*...) while((s32[]{:T(128)}, f32[64,8,512]{2,1,0:T(8,128)S(1)}, ...), condition=%wide.region_12.13_spmd, body=%wide.region_11.12_spmd.sunk | while | flops 1210318848 | bytes 12976363 | solution.py:41
  274.4 1.6 fusion.83
  276.0 4.2 fusion.84
  280.2 1.6 fusion.83
  281.8 4.2 fusion.84
  286.0 1.6 fusion.83
  287.6 4.2 fusion.84
  291.8 1.6 fusion.83
  293.5 4.2 fusion.84
  297.7 0.0 copy-start.1
  297.7 1.0 copy-done.1
  298.6 0.0 reduce-scatter.9.cloned.1.call-update
  298.6 0.0 reduce-scatter.11.cloned.1.call-start
  298.7 40.1 %reduce-scatter.9.cloned.1.call-done = f32[64,8,256]{2,1,0:T(8,128)} async-done(((f32[64,8,512]{2,1,0:T(8,128)}), f32[64,8,256]{2,1,0:T(8,128)}) %reduce-scatter.9.cloned.1.call-update) | async-done | bytes 524304 | tf_op jit(solution)/shard_map/reduce_scatter | solution.py:42
  338.8 0.0 reduce-scatter.11.cloned.1.call-update
  338.8 0.0 all-reduce.5.cloned.1.call-start
  338.9 76.0 %psum.38 = bf16[8,512]{1,0:T(8,128)(2,1)S(1)} all-reduce(f32[8,512]{1,0:T(8,128)S(1)} %get-tuple-element.308), channel_id=1, replica_groups=mesh['grp'=2,'aux'=8,'tr'=2] {'aux','tr'}, use_global_device_ids=true, to_apply=%region_17.18 | all-reduce | flops 4096 | bytes 24576 | tf_op jit(solution)/shard_map/psum | solution.py:50
  414.9 0.0 reduce-scatter.11.cloned.1.call-done
  414.9 1.5 add.79
  416.4 0.0 all-reduce.5.cloned.1.call-update
  416.5 0.7 copy.10
  417.1 13.1 %all-reduce.5.cloned.1.call-done = f32[8,8,256]{2,1,0:T(8,128)} async-done(((f32[8,8,256]{2,1,0:T(8,128)}), f32[8,8,256]{2,1,0:T(8,128)}) %all-reduce.5.cloned.1.call-update) | async-done | bytes 65552 | tf_op jit(solution)/shard_map/psum | solution.py:59
  430.2 1.5 multiply_add_fusion
  (17 shorter events, 0.1 us)
Async XLA Ops:
  7.2 100.8 %reduce-scatter.5.cloned.1.call-start = ((), (), s32[]{:S(2)}) async-start(), calls=%async_computation.4 | async-start | bytes 1572864 | tf_op jit(solution)/shard_map/reduce_scatter | solution.py:42
  41.4 66.7 %copy-start = (bf16[8,256,512]{2,1,0:T(8,128)(2,1)S(1)}, bf16[8,256,512]{2,1,0:T(8,128)(2,1)}, u32[]{:S(2)}) copy-start(bf16[8,256,512]{2,1,0:T(8,128)(2,1)} %param.24) | copy-start | bytes 6291460
  64.9 1.0 copy-start.2
  65.8 118.2 %reduce-scatter.7.cloned.1.call-start = ((), (), s32[]{:S(2)}) async-start(), calls=%async_computation.5 | async-start | bytes 589824 | tf_op jit(solution)/shard_map/reduce_scatter | solution.py:43
  108.0 91.3 %all-reduce.3.cloned.1.call-start = ((), (), s32[]{:S(2)}) async-start(), calls=%async_computation.6 | async-start | bytes 131072 | tf_op jit(solution)/shard_map/psum | solution.py:59
  108.1 77.5 %copy-start.4 = (f32[256]{0:T(256)S(1)}, f32[256]{0:T(256)}, u32[]{:S(2)}) copy-start(f32[256]{0:T(256)} %param.21) | copy-start | bytes 3076
  108.1 77.5 %copy-start.5 = (f32[8]{0:T(128)S(1)}, f32[8]{0:T(128)}, u32[]{:S(2)}) copy-start(f32[8]{0:T(128)} %param.20) | copy-start | bytes 100
  108.1 91.2 %copy-start.3 = (f32[8,8,256]{2,1,0:T(8,128)S(1)}, f32[8,8,256]{2,1,0:T(8,128)}, u32[]{:S(2)}) copy-start(f32[8,8,256]{2,1,0:T(8,128)} %param.19) | copy-start | bytes 196612
  185.5 153.3 %reduce-scatter.9.cloned.1.call-start = ((), (), s32[]{:S(2)}) async-start(), calls=%async_computation.7 | async-start | bytes 1572864 | tf_op jit(solution)/shard_map/reduce_scatter | solution.py:42
  297.7 1.0 copy-start.1
  298.6 116.3 %reduce-scatter.11.cloned.1.call-start = ((), (), s32[]{:S(2)}) async-start(), calls=%async_computation.8 | async-start | bytes 589824 | tf_op jit(solution)/shard_map/reduce_scatter | solution.py:43
  338.8 91.3 %all-reduce.5.cloned.1.call-start = ((), (), s32[]{:S(2)}) async-start(), calls=%async_computation.9 | async-start | bytes 131072 | tf_op jit(solution)/shard_map/psum | solution.py:59
Sparse Core Ops, SparseCore 0:
  66.0 41.9 reduce-scatter.4
  111.3 62.7 reduce-scatter.6
  185.6 13.5 all-reduce.2
  298.8 39.9 reduce-scatter.8
  342.0 62.8 reduce-scatter.10
  416.6 13.5 all-reduce.4
where the time goes:
time: 437 us; the launch traced here: 439 us
  blocking collectives  257 us (59%)
  waiting for transfers between devices  109 us (25%)
  matrix products  48.4 us (11%)
  between operations  14.9 us (3%)
  other arithmetic  5.41 us (1%)
    psum x2, blocking collectives, apply_hamiltonian(): projection = lax.psum(projection, ('aux', 'tr'))  152 us
    reduce_scatter x2, waiting for transfers between devices, apply_hamiltonian(): lax.psum_scatter(direct_term, 'tr', scatter_dimension=2, tiled=True)  82.2 us
    all_gather x2, blocking collectives, apply_hamiltonian(): gathered = lax.all_gather(rounded, 'aux', axis=0, tiled=True)  63.3 us
    psum x1, blocking collectives, body(): intersection = lax.psum(partial_intersection, ('aux', 'tr')) / (V * C)  42.1 us
    dot_general x8, matrix products, one_block(): jnp.einsum('pukc,pcd->ukd', blended, piece_virt, preferred_element_type=j...  33.5 us
    psum x2, waiting for transfers between devices, apply_hamiltonian(): combined = lax.psum(direct_term + exchange_term, 'grp')  26.7 us
    dot_general x8, matrix products, one_block(): jnp.einsum('puv,vkc->pukc', piece_occ, gathered, preferred_element_type=j...  12.9 us
  transfers between devices with their start and end apart: 6, of which 4 were waited for; matrix products, arithmetic and copies ran while one was open for 0% of the time, Pallas kernels for 0%

commit v1 on v0

v1 whole, which is shorter than its diff:
```python
import functools

import jax
import jax.numpy as jnp
from jax import lax
from jax.experimental import pallas as pl
from jax.experimental.pallas import tpu as pltpu
from jax.sharding import PartitionSpec as P

F32 = jnp.float32
BF16 = jnp.bfloat16
MESH = pl.DeviceIdType.MESH


def kernel(
    naux, ntr, chunk,
    live_ref, trial_ref, val_ref, cond_ref, occ_hbm, virt_hbm, pair_hbm,
    out_ref, inter_ref,
    occ, virt, pair, blended, acc, wide, mixed,
    block_send, block_recv, proj_send, proj_recv, tr_send, tr_recv,
    sum_send, sum_recv, dots_send, dots_recv, core_recv, final_send, final_recv,
    load_sem, virt_sem, block_ssem, block_rsem, proj_ssem, proj_rsem,
    tr_ssem, tr_rsem, sum_ssem, sum_rsem, dots_ssem, dots_rsem, core_ssem, core_rsem,
):
    g = lax.axis_index("grp")
    a = lax.axis_index("aux")
    t = lax.axis_index("tr")
    vectors, own_val, cond = trial_ref.shape
    half = vectors // 2
    slots, val, _ = occ.shape
    chunks = slots // chunk
    other_t = lax.rem(t + 1, ntr)
    own_cols = pl.ds(pl.multiple_of(t * cond, cond), cond)
    other_cols = pl.ds(pl.multiple_of(other_t * cond, cond), cond)

    occ_copy = pltpu.make_async_copy(occ_hbm, occ, load_sem.at[0])
    pair_copy = pltpu.make_async_copy(pair_hbm, pair, load_sem.at[1])
    occ_copy.start()
    pair_copy.start()

    def virt_copy(i):
        part = pl.ds(i * chunk, chunk)
        return pltpu.make_async_copy(virt_hbm.at[part], virt.at[part], virt_sem.at[i])

    for i in range(chunks):
        virt_copy(i).start()

    everyone = [(da, dt) for da in range(naux) for dt in range(ntr) if (da, dt) != (0, 0)]

    def peer(da, dt):
        return {"aux": lax.rem(a + da, naux), "tr": lax.rem(t + dt, ntr)}

    barrier = pltpu.get_barrier_semaphore()
    for da, dt in everyone:
        pl.semaphore_signal(barrier, inc=1, device_id=peer(da, dt), device_id_type=MESH)
    pl.semaphore_signal(barrier, inc=1, device_id={"grp": 1 - g}, device_id_type=MESH)

    gap = cond_ref[...] - val_ref[...]

    def to_all(it, send, recv, ssem, rsem):
        copies = []
        for da, dt in everyone:
            n = da * ntr + dt
            copies.append(pltpu.make_async_remote_copy(
                src_ref=send.at[it], dst_ref=recv.at[it, n],
                send_sem=ssem.at[it, n], recv_sem=rsem.at[it, n],
                device_id=peer(da, dt), device_id_type=MESH))
        return copies

    def apply(it, x):
        block = jnp.concatenate(x, axis=1).astype(BF16)
        block_send[it] = block
        block_recv[it, a] = block
        if it == 0:
            pl.semaphore_wait(barrier, len(everyone) + 1)
        gathers = []
        for d in range(1, naux):
            copy = pltpu.make_async_remote_copy(
                src_ref=block_send.at[it], dst_ref=block_recv.at[it, a],
                send_sem=block_ssem.at[it, d], recv_sem=block_rsem.at[it, d],
                device_id=peer(d, 0), device_id_type=MESH)
            copy.start()
            gathers.append(copy)

        if it == 0:
            pair_copy.wait()
        for k in range(half):
            mixed[:, k, :] = x[k]
        proj = jnp.zeros((half, pair.shape[2]), F32)
        for v in range(own_val):
            proj += jnp.dot(mixed[v].astype(BF16), pair[v], preferred_element_type=F32)
        proj_send[it] = proj
        projections = to_all(it, proj_send, proj_recv, proj_ssem, proj_rsem)
        for copy in projections:
            copy.start()

        if it == 0:
            occ_copy.wait()
            live = live_ref[0, 0]

            @pl.loop(0, slots)
            def _(p):
                keep = (p < live).astype(F32)
                occ[p] = (occ[p].astype(F32) * keep).astype(BF16)

        for copy in gathers:
            copy.wait_recv()
        for s in range(naux):
            wide[pl.ds(s * own_val, own_val), :] = block_recv[it, s].astype(F32)
        gathered = [wide[:, k * cond:(k + 1) * cond].astype(BF16) for k in range(half)]
        acc[...] = jnp.zeros_like(acc)

        @pl.loop(0, chunks)
        def _(i):
            if it == 0:
                virt_copy(i).wait()
            part = pl.ds(i * chunk, chunk)
            occ_part = occ[part].reshape(chunk * val, val)
            for k in range(half):
                b = jnp.dot(occ_part, gathered[k], preferred_element_type=F32).astype(BF16)
                for q in range(chunk):
                    blended[i, k * val:(k + 1) * val, q * cond:(q + 1) * cond] = b[q * val:(q + 1) * val]
            acc[...] += jnp.dot(
                blended[i], virt[part, :, other_cols].reshape(chunk * cond, cond),
                preferred_element_type=F32)

        tr_send[it] = acc[...].astype(BF16)
        tr_copy = pltpu.make_async_remote_copy(
            src_ref=tr_send.at[it], dst_ref=tr_recv.at[it],
            send_sem=tr_ssem.at[it], recv_sem=tr_rsem.at[it],
            device_id=peer(0, 1), device_id_type=MESH)
        tr_copy.start()
        acc[...] = jnp.zeros_like(acc)

        @pl.loop(0, chunks)
        def _(i):
            part = pl.ds(i * chunk, chunk)
            acc[...] += jnp.dot(
                blended[i], virt[part, :, own_cols].reshape(chunk * cond, cond),
                preferred_element_type=F32)

        tr_copy.wait_recv()
        acc[...] += tr_recv[it].astype(F32)
        for s in range(naux):
            for k in range(half):
                row = k * val + s * own_val
                sum_send[it, s, :, k * cond:(k + 1) * cond] = acc[row:row + own_val, :].astype(BF16)
        sums = []
        for d in range(1, naux):
            copy = pltpu.make_async_remote_copy(
                src_ref=sum_send.at[it, lax.rem(a + d, naux)], dst_ref=sum_recv.at[it, d],
                send_sem=sum_ssem.at[it, d], recv_sem=sum_rsem.at[it, d],
                device_id=peer(d, 0), device_id_type=MESH)
            copy.start()
            sums.append(copy)

        for copy in projections:
            copy.wait_recv()
        proj = proj_send[it]
        for da, dt in everyone:
            proj += proj_recv[it, da * ntr + dt]
        proj_b = proj.astype(BF16)
        for v in range(own_val):
            mixed[v] = lax.dot_general(
                proj_b, pair[v], (((1,), (1,)), ((), ())), preferred_element_type=F32)
        total = sum_send[it, a].astype(F32)
        for copy in sums:
            copy.wait_recv()
        for d in range(1, naux):
            total += sum_recv[it, d].astype(F32)
        result = []
        for k in range(half):
            result.append(gap * x[k] + total[:, k * cond:(k + 1) * cond] + mixed[:, k, :])
        for copy in gathers + projections + sums + [tr_copy]:
            copy.wait_send()
        return result

    first = apply(0, [trial_ref[g * half + k] for k in range(half)])

    trial = trial_ref[...]
    lanes = lax.broadcasted_iota(jnp.int32, (vectors, 128), 1)
    partial = jnp.zeros((vectors, 128), F32)
    for j in range(half):
        lanewise = jnp.sum(trial * first[j][None], axis=1)
        column = jnp.sum(lanewise, axis=1, keepdims=True)
        partial += jnp.where(lanes == g * half + j, column, 0.0)
    dots_send[0] = partial
    dots = to_all(0, dots_send, dots_recv, dots_ssem, dots_rsem)
    for copy in dots:
        copy.start()
    for copy in dots:
        copy.wait()
    by_tile = dots_recv[0, 0 + 1]
    for da, dt in everyone[1:]:
        by_tile += dots_recv[0, da * ntr + dt]
    inter = (by_tile + partial) / (naux * own_val * ntr * cond)
    dots_send[1] = inter
    core_dots = pltpu.make_async_remote_copy(
        src_ref=dots_send.at[1], dst_ref=core_recv,
        send_sem=core_ssem.at[0], recv_sem=core_rsem.at[0],
        device_id={"grp": 1 - g}, device_id_type=MESH)
    core_dots.start()

    correction = []
    for j in range(half):
        column = jnp.sum(jnp.where(lanes == g * half + j, inter, 0.0), axis=1, keepdims=True)
        fitted = trial_ref[0] * column[0:1, :]
        for k in range(1, vectors):
            fitted += trial_ref[k] * column[k:k + 1, :]
        correction.append((first[j] - fitted) / gap)

    second = apply(1, correction)
    for k in range(half):
        final_send[k] = second[k]
        out_ref[g * half + k] = second[k]
    final_copy = pltpu.make_async_remote_copy(
        src_ref=final_send, dst_ref=final_recv,
        send_sem=core_ssem.at[1], recv_sem=core_rsem.at[1],
        device_id={"grp": 1 - g}, device_id_type=MESH)
    final_copy.start()
    core_dots.wait()
    inter_ref[...] = (dots_send[1] + core_recv[...])[:, :vectors]
    final_copy.wait()
    for k in range(half):
        out_ref[(1 - g) * half + k] = final_recv[k]


def body(naux, ntr, trial_vectors, energy_val, energy_cond, coef_occ, coef_virt, pair_coef, live_aux):
    own_val, vectors, cond = trial_vectors.shape
    slots, val, _ = coef_occ.shape
    naux_all = pair_coef.shape[2]
    half = vectors // 2
    chunk = 8
    peers = naux * ntr
    vmem = pl.BlockSpec(memory_space=pltpu.VMEM)
    hbm = pl.BlockSpec(memory_space=pl.ANY)
    dma = pltpu.SemaphoreType.DMA
    scratch = [
        pltpu.VMEM(coef_occ.shape, BF16),
        pltpu.VMEM(coef_virt.shape, BF16),
        pltpu.VMEM(pair_coef.shape, BF16),
        pltpu.VMEM((slots // chunk, half * val, chunk * cond), BF16),
        pltpu.VMEM((half * val, cond), F32),
        pltpu.VMEM((val, half * cond), F32),
        pltpu.VMEM((own_val, half, cond), F32),
        pltpu.VMEM((2, own_val, half * cond), BF16),
        pltpu.VMEM((2, naux, own_val, half * cond), BF16),
        pltpu.VMEM((2, half, naux_all), F32),
        pltpu.VMEM((2, peers, half, naux_all), F32),
        pltpu.VMEM((2, half * val, cond), BF16),
        pltpu.VMEM((2, half * val, cond), BF16),
        pltpu.VMEM((2, naux, own_val, half * cond), BF16),
        pltpu.VMEM((2, naux, own_val, half * cond), BF16),
        pltpu.VMEM((2, vectors, 128), F32),
        pltpu.VMEM((1, peers, vectors, 128), F32),
        pltpu.VMEM((vectors, 128), F32),
        pltpu.VMEM((half, own_val, cond), F32),
        pltpu.VMEM((half, own_val, cond), F32),
        dma((2,)), dma((slots // chunk,)),
        dma((2, naux)), dma((2, naux)),
        dma((2, peers)), dma((2, peers)),
        dma((2,)), dma((2,)),
        dma((2, naux)), dma((2, naux)),
        dma((1, peers)), dma((1, peers)),
        dma((2,)), dma((2,)),
    ]
    applied, intersection = pl.pallas_call(
        functools.partial(kernel, naux, ntr, chunk),
        out_shape=(
            jax.ShapeDtypeStruct((vectors, own_val, cond), F32),
            jax.ShapeDtypeStruct((vectors, vectors), F32),
        ),
        in_specs=[pl.BlockSpec(memory_space=pltpu.SMEM), vmem, vmem, vmem, hbm, hbm, hbm],
        out_specs=(vmem, vmem),
        scratch_shapes=scratch,
        compiler_params=pltpu.CompilerParams(
            collective_id=0, has_side_effects=True, vmem_limit_bytes=56 * 1024 * 1024
        ),
    )(
        live_aux.reshape(1, 1), trial_vectors.transpose(1, 0, 2), energy_val.reshape(-1, 1),
        energy_cond.reshape(1, -1), coef_occ, coef_virt, pair_coef,
    )
    return applied.transpose(1, 0, 2), intersection


def solution(mesh):
    in_specs = (
        P("aux", None, "tr"),
        P("aux"),
        P("tr"),
        P("aux", None, None),
        P("aux", "tr", None),
        P("aux", "tr", None),
        P("aux"),
    )
    out_specs = (P("aux", None, "tr"), P())
    sizes = (mesh.shape["aux"], mesh.shape["tr"])
    return jax.shard_map(
        functools.partial(body, *sizes), mesh=mesh, in_specs=in_specs, out_specs=out_specs, check_vma=False
    )
```

time: 437 us -> 69.1 us (0.16)
  blocking collectives: 257 us -> 0 us
  waiting for transfers between devices: 109 us -> 0 us
  Pallas kernels: 0 us -> 61.9 us
  matrix products: 48.4 us -> 0 us
  between operations: 14.9 us -> 1.29 us
  other arithmetic: 5.41 us -> 0 us
    psum x3 -> x0, blocking collectives: 194 us -> none  [the longest x2 152 us: apply_hamiltonian(): projection = lax.psum(projection, ('aux', 'tr'))]
    reduce_scatter x4 -> x0, waiting for transfers between devices: 82.2 us -> none  [the longest x2 82.2 us: apply_hamiltonian(): lax.psum_scatter(direct_term, 'tr', scatter_dimension=2, tiled=True)]
    all_gather x2 -> x0, blocking collectives: 63.3 us -> none  [apply_hamiltonian(): gathered = lax.all_gather(rounded, 'aux', axis=0, tiled=True)]
    pallas_call x0 -> x1, Pallas kernels: none -> 61.9 us  [body(): pl.pallas_call(functools.partial(kernel, naux, ntr, chunk), out_shape=(ja...]
    dot_general x18 -> x0, matrix products: 48.4 us -> none  [the longest x8 33.5 us: one_block(): jnp.einsum('pukc,pcd->ukd', blended, piece_virt, preferred_element_type=j...]
    psum x2 -> x0, waiting for transfers between devices: 26.7 us -> none  [apply_hamiltonian(): combined = lax.psum(direct_term + exchange_term, 'grp')]
    add x3 -> x0, other arithmetic: 4.44 us -> none  [the longest x2 2.96 us: apply_hamiltonian(): combined = lax.psum(direct_term + exchange_term, 'grp')]
  transfers between devices with their start and end apart: 6 -> 0, of which waited for: 4 -> 0; matrix products, arithmetic and copies ran while one was open for 0% -> 0% of each run, Pallas kernels for 0% -> 0%
where the time goes in v1:
time: 69.1 us; the launch traced here: 68.8 us
  Pallas kernels  61.9 us (90%)
  local copies, waits for them, and re-layouts  5.58 us (8%)
  between operations  1.29 us (2%)
    pallas_call x1, Pallas kernels, body(): pl.pallas_call(functools.partial(kernel, naux, ntr, chunk), out_shape=(ja...  61.9 us
    unnamed x3, local copies, waits for them, and re-layouts  4.25 us

profile of v1, /device:TPU:0, one launch (start us, length us, event | category | flops | bytes accessed | tf_op | source)
XLA Modules:
  0.0 68.8 jit_solution(14469866442284001856)
XLA Ops:
  1.3 1.3 %copy.10.val_ref = f32[8,1]{1,0:T(8,128)} copy(f32[8,1]{0,1:T(1,128)} %bitcast.11) | data formatting | bytes 64 | tf_op jit(solution)/shard_map/reshape | solution.py:280
  2.6 1.5 %copy.13 = f32[8,8,256]{2,0,1:T(8,128)} copy(f32[8,8,256]{2,1,0:T(8,128)} %param.7) | data formatting | bytes 131072 | tf_op args[0]
  4.1 61.9 %shard_map.86 = (f32[8,8,256]{2,1,0:T(8,128)}, f32[8,8]{1,0:T(8,128)}) custom-call(s32[1,1]{1,0:T(1,128)} %bitcast.7.live_ref, f32[8,8,256]{2,1,0:T(8,128)} %bitcast.8, f32[8,1]{1,0:T(8,128)} %copy.10.val_ref, f32[1,256]{1,0:T(1,128)} %bitcast.10, bf16[64,64,64]{2,1,0:T(8,128)(2,1)} %occ_hbm.1, bf16[64,256,512]{2,1,0:T(8,128)(2,1)} %virt_hbm.1, ...), custom_call_target="tpu_custom_call" | custom-call | tf_op jit(solution)/shard_map/pallas_call | solution.py:267
  66.0 1.5 %copy.11 = f32[8,8,256]{2,1,0:T(8,128)} copy(f32[8,8,256]{2,0,1:T(8,128)} %bitcast.9) | data formatting | bytes 131072
  67.5 1.3 %copy.16 = f32[8,8]{1,0:T(8,128)} copy(f32[8,8]{1,0:T(8,128)} %get-tuple-element.11) | data formatting | bytes 512

commit v2 on v1

v2 whole, which is shorter than its diff:
```python
import functools

import jax
import jax.numpy as jnp
from jax import lax
from jax.experimental import pallas as pl
from jax.experimental.pallas import tpu as pltpu
from jax.sharding import PartitionSpec as P

F32 = jnp.float32
BF16 = jnp.bfloat16
GROUPS = 1
MESH = pl.DeviceIdType.MESH


def kernel(
    naux, ntr, groups,
    live_ref, trial_ref, val_ref, cond_ref, occ_hbm, virt_hbm, pair_hbm,
    out_ref, inter_ref,
    occ, virt, pair, blended, acc, wide, mixed, trial_k,
    block_send, block_recv, proj_send, proj_recv, tr_send, tr_recv,
    sum_send, sum_recv, dots_send, dots_recv, core_recv, final_send, final_recv,
    load_sem, block_ssem, block_rsem, proj_ssem, proj_rsem,
    tr_ssem, tr_rsem, sum_ssem, sum_rsem, dots_ssem, dots_rsem, core_ssem, core_rsem,
):
    g = lax.axis_index("grp")
    a = lax.axis_index("aux")
    t = lax.axis_index("tr")
    own_val, vectors, cond = trial_ref.shape
    half = vectors // 2
    size = half // groups
    slots, val, _ = occ.shape
    other_t = lax.rem(t + 1, ntr)
    own_cols = pl.ds(pl.multiple_of(t * cond, cond), cond)
    other_cols = pl.ds(pl.multiple_of(other_t * cond, cond), cond)

    occ_copy = pltpu.make_async_copy(occ_hbm, occ, load_sem.at[0])
    pair_copy = pltpu.make_async_copy(pair_hbm, pair, load_sem.at[1])
    occ_copy.start()
    pair_copy.start()

    virt_copy = pltpu.make_async_copy(virt_hbm, virt, load_sem.at[2])
    virt_copy.start()

    everyone = [(da, dt) for da in range(naux) for dt in range(ntr) if (da, dt) != (0, 0)]

    def peer(da, dt):
        return {"aux": lax.rem(a + da, naux), "tr": lax.rem(t + dt, ntr)}

    barrier = pltpu.get_barrier_semaphore()
    for da, dt in everyone:
        pl.semaphore_signal(barrier, inc=1, device_id=peer(da, dt), device_id_type=MESH)
    pl.semaphore_signal(barrier, inc=1, device_id={"grp": 1 - g}, device_id_type=MESH)

    square = (own_val, own_val)
    diagonal = lax.broadcasted_iota(jnp.int32, square, 0) == lax.broadcasted_iota(jnp.int32, square, 1)
    val_column = jnp.sum(jnp.where(diagonal, val_ref[...], 0.0), axis=1, keepdims=True)
    gap = cond_ref[...] - val_column
    for k in range(vectors):
        trial_k[k] = trial_ref[:, k, :]

    def to_all(it, send, recv, ssem, rsem):
        copies = []
        for da, dt in everyone:
            n = da * ntr + dt
            copies.append(pltpu.make_async_remote_copy(
                src_ref=send.at[it], dst_ref=recv.at[it, n],
                send_sem=ssem.at[it, n], recv_sem=rsem.at[it, n],
                device_id=peer(da, dt), device_id_type=MESH))
        return copies

    def apply(it, x):
        for r in range(groups):
            block = jnp.concatenate(x[r * size:(r + 1) * size], axis=1).astype(BF16)
            block_send[it, r] = block
            block_recv[it, r, a] = block
        if it == 0:
            pl.semaphore_wait(barrier, len(everyone) + 1)
        gathers = []
        for r in range(groups):
            gathers.append([])
            for d in range(1, naux):
                copy = pltpu.make_async_remote_copy(
                    src_ref=block_send.at[it, r], dst_ref=block_recv.at[it, r, a],
                    send_sem=block_ssem.at[it, r, d], recv_sem=block_rsem.at[it, r, d],
                    device_id=peer(d, 0), device_id_type=MESH)
                copy.start()
                gathers[r].append(copy)

        if it == 0:
            pair_copy.wait()
        for k in range(half):
            mixed[:, k, :] = x[k]
        proj = jnp.zeros((half, pair.shape[2]), F32)
        for v in range(own_val):
            proj += jnp.dot(mixed[v].astype(BF16), pair[v], preferred_element_type=F32)
        proj_send[it] = proj
        projections = to_all(it, proj_send, proj_recv, proj_ssem, proj_rsem)
        for copy in projections:
            copy.start()

        if it == 0:
            occ_copy.wait()
            live = live_ref[...]

            @pl.loop(0, slots)
            def _(p):
                keep = (p < live).astype(F32)
                occ[p] = (occ[p].astype(F32) * keep).astype(BF16)

        tr_copies = []
        for r in range(groups):
            for copy in gathers[r]:
                copy.wait_recv()
            for s in range(naux):
                wide[pl.ds(s * own_val, own_val), :] = block_recv[it, r, s].astype(F32)
            rows = occ[...].reshape(slots * val, val)
            for k in range(size):
                column = wide[:, k * cond:(k + 1) * cond].astype(BF16)
                b = jnp.dot(rows, column, preferred_element_type=F32).astype(BF16)
                for q in range(slots):
                    blended[r, k * val:(k + 1) * val, q * cond:(q + 1) * cond] = b[q * val:(q + 1) * val]
            if it == 0 and r == 0:
                virt_copy.wait()
            tr_send[it, r] = jnp.dot(
                blended[r], virt[:, :, other_cols].reshape(slots * cond, cond),
                preferred_element_type=F32).astype(BF16)
            copy = pltpu.make_async_remote_copy(
                src_ref=tr_send.at[it, r], dst_ref=tr_recv.at[it, r],
                send_sem=tr_ssem.at[it, r], recv_sem=tr_rsem.at[it, r],
                device_id=peer(0, 1), device_id_type=MESH)
            copy.start()
            tr_copies.append(copy)

        sums = []
        for r in range(groups):
            acc[...] = jnp.dot(
                blended[r], virt[:, :, own_cols].reshape(slots * cond, cond),
                preferred_element_type=F32)
            tr_copies[r].wait_recv()
            acc[...] += tr_recv[it, r].astype(F32)
            for s in range(naux):
                for k in range(size):
                    row = k * val + s * own_val
                    sum_send[it, r, s, :, k * cond:(k + 1) * cond] = acc[row:row + own_val, :].astype(BF16)
            for d in range(1, naux):
                copy = pltpu.make_async_remote_copy(
                    src_ref=sum_send.at[it, r, lax.rem(a + d, naux)], dst_ref=sum_recv.at[it, r, d],
                    send_sem=sum_ssem.at[it, r, d], recv_sem=sum_rsem.at[it, r, d],
                    device_id=peer(d, 0), device_id_type=MESH)
                copy.start()
                sums.append(copy)

        for copy in projections:
            copy.wait_recv()
        proj = proj_send[it]
        for da, dt in everyone:
            proj += proj_recv[it, da * ntr + dt]
        proj_b = proj.astype(BF16)
        for v in range(own_val):
            mixed[v] = lax.dot_general(
                proj_b, pair[v], (((1,), (1,)), ((), ())), preferred_element_type=F32)
        for copy in sums:
            copy.wait_recv()
        result = []
        for r in range(groups):
            total = sum_send[it, r, a].astype(F32)
            for d in range(1, naux):
                total += sum_recv[it, r, d].astype(F32)
            for k in range(size):
                n = r * size + k
                result.append(gap * x[n] + total[:, k * cond:(k + 1) * cond] + mixed[:, n, :])
        for copy in [c for part in gathers for c in part] + projections + sums + tr_copies:
            copy.wait_send()
        return result

    first = apply(0, [trial_k[g * half + k] for k in range(half)])

    trial = trial_k[...]
    lanes = lax.broadcasted_iota(jnp.int32, (vectors, 128), 1)
    partial = jnp.zeros((vectors, 128), F32)
    for j in range(half):
        lanewise = jnp.sum(trial * first[j][None], axis=1)
        column = jnp.sum(lanewise, axis=1, keepdims=True)
        partial += jnp.where(lanes == g * half + j, column, 0.0)
    dots_send[0] = partial
    dots = to_all(0, dots_send, dots_recv, dots_ssem, dots_rsem)
    for copy in dots:
        copy.start()
    for copy in dots:
        copy.wait()
    for da, dt in everyone:
        partial += dots_recv[0, da * ntr + dt]
    inter = partial / (naux * own_val * ntr * cond)
    dots_send[1] = inter
    core_dots = pltpu.make_async_remote_copy(
        src_ref=dots_send.at[1], dst_ref=core_recv,
        send_sem=core_ssem.at[0], recv_sem=core_rsem.at[0],
        device_id={"grp": 1 - g}, device_id_type=MESH)
    core_dots.start()

    correction = []
    for j in range(half):
        column = jnp.sum(jnp.where(lanes == g * half + j, inter, 0.0), axis=1, keepdims=True)
        fitted = trial_k[0] * column[0:1, :]
        for k in range(1, vectors):
            fitted += trial_k[k] * column[k:k + 1, :]
        correction.append((first[j] - fitted) / gap)

    second = apply(1, correction)
    for k in range(half):
        final_send[k] = second[k]
        out_ref[g * half + k] = second[k]
    final_copy = pltpu.make_async_remote_copy(
        src_ref=final_send, dst_ref=final_recv,
        send_sem=core_ssem.at[1], recv_sem=core_rsem.at[1],
        device_id={"grp": 1 - g}, device_id_type=MESH)
    final_copy.start()
    core_dots.wait()
    inter_ref[...] = (dots_send[1] + core_recv[...])[:, :vectors]
    final_copy.wait()
    for k in range(half):
        out_ref[(1 - g) * half + k] = final_recv[k]


def finish(applied_ref, inter_ref, out_ref, inter_out_ref):
    for k in range(applied_ref.shape[0]):
        out_ref[:, k, :] = applied_ref[k]
    inter_out_ref[...] = inter_ref[...]


def body(naux, ntr, trial_vectors, energy_val, energy_cond, coef_occ, coef_virt, pair_coef, live_aux):
    own_val, vectors, cond = trial_vectors.shape
    slots, val, _ = coef_occ.shape
    naux_all = pair_coef.shape[2]
    half = vectors // 2
    groups = GROUPS
    size = half // groups
    peers = naux * ntr
    vmem = pl.BlockSpec(memory_space=pltpu.VMEM)
    hbm = pl.BlockSpec(memory_space=pl.ANY)
    dma = pltpu.SemaphoreType.DMA
    scratch = [
        pltpu.VMEM(coef_occ.shape, BF16),
        pltpu.VMEM(coef_virt.shape, BF16),
        pltpu.VMEM(pair_coef.shape, BF16),
        pltpu.VMEM((groups, size * val, slots * cond), BF16),
        pltpu.VMEM((size * val, cond), F32),
        pltpu.VMEM((val, size * cond), F32),
        pltpu.VMEM((own_val, half, cond), F32),
        pltpu.VMEM((vectors, own_val, cond), F32),
        pltpu.VMEM((2, groups, own_val, size * cond), BF16),
        pltpu.VMEM((2, groups, naux, own_val, size * cond), BF16),
        pltpu.VMEM((2, half, naux_all), F32),
        pltpu.VMEM((2, peers, half, naux_all), F32),
        pltpu.VMEM((2, groups, size * val, cond), BF16),
        pltpu.VMEM((2, groups, size * val, cond), BF16),
        pltpu.VMEM((2, groups, naux, own_val, size * cond), BF16),
        pltpu.VMEM((2, groups, naux, own_val, size * cond), BF16),
        pltpu.VMEM((2, vectors, 128), F32),
        pltpu.VMEM((1, peers, vectors, 128), F32),
        pltpu.VMEM((vectors, 128), F32),
        pltpu.VMEM((half, own_val, cond), F32),
        pltpu.VMEM((half, own_val, cond), F32),
        dma((3,)),
        dma((2, groups, naux)), dma((2, groups, naux)),
        dma((2, peers)), dma((2, peers)),
        dma((2, groups)), dma((2, groups)),
        dma((2, groups, naux)), dma((2, groups, naux)),
        dma((1, peers)), dma((1, peers)),
        dma((2,)), dma((2,)),
    ]
    applied, intersection = pl.pallas_call(
        functools.partial(kernel, naux, ntr, groups),
        out_shape=(
            jax.ShapeDtypeStruct((vectors, own_val, cond), F32),
            jax.ShapeDtypeStruct((vectors, vectors), F32),
        ),
        in_specs=[vmem, vmem, vmem, vmem, hbm, hbm, hbm],
        out_specs=(vmem, vmem),
        scratch_shapes=scratch,
        compiler_params=pltpu.CompilerParams(
            collective_id=0, has_side_effects=True, vmem_limit_bytes=56 * 1024 * 1024
        ),
    )(
        live_aux.reshape(1, 1), trial_vectors, energy_val.reshape(1, -1),
        energy_cond.reshape(1, -1), coef_occ, coef_virt, pair_coef,
    )
    return pl.pallas_call(
        finish,
        out_shape=(
            jax.ShapeDtypeStruct(trial_vectors.shape, F32),
            jax.ShapeDtypeStruct((vectors, vectors), F32),
        ),
        in_specs=[vmem, vmem],
        out_specs=(vmem, vmem),
    )(applied, intersection)


def solution(mesh):
    in_specs = (
        P("aux", None, "tr"),
        P("aux"),
        P("tr"),
        P("aux", None, None),
        P("aux", "tr", None),
        P("aux", "tr", None),
        P("aux"),
    )
    out_specs = (P("aux", None, "tr"), P())
    sizes = (mesh.shape["aux"], mesh.shape["tr"])
    return jax.shard_map(
        functools.partial(body, *sizes), mesh=mesh, in_specs=in_specs, out_specs=out_specs, check_vma=False
    )
```

time: 69.1 us -> 61.1 us (0.88)
  local copies, waits for them, and re-layouts: 5.58 us -> 0 us
  Pallas kernels: 61.9 us -> 59.6 us
    unnamed x3 -> x0, local copies, waits for them, and re-layouts: 4.25 us -> none
    pallas_call x1 -> x2, Pallas kernels: 61.9 us -> 59.6 us  [the longest x1 58.1 us: body(): pl.pallas_call(functools.partial(kernel, naux, ntr, groups), out_shape=(j...]
    reshape x1 -> x0, local copies, waits for them, and re-layouts: 1.32 us -> none  [body(): energy_val.reshape(-1, 1)]
where the time goes in v2:
time: 61.1 us; the launch traced here: 60.9 us
  Pallas kernels  59.6 us (98%)
  between operations  1.29 us (2%)
    pallas_call x1, Pallas kernels, body(): pl.pallas_call(functools.partial(kernel, naux, ntr, groups), out_shape=(j...  58.1 us
    pallas_call x1, Pallas kernels, body(): pl.pallas_call(finish, out_shape=(jax.ShapeDtypeStruct(trial_vectors.shap...  1.5 us

profile of v2, /device:TPU:0, one launch (start us, length us, event | category | flops | bytes accessed | tf_op | source)
XLA Modules:
  0.0 60.9 jit_solution(12751805482484736381)
XLA Ops:
  1.3 58.1 %shard_map.86 = (f32[8,8,256]{2,1,0:T(8,128)}, f32[8,8]{1,0:T(8,128)}) custom-call(s32[1,1]{1,0:T(1,128)} %bitcast.3.live_ref, f32[8,8,256]{2,1,0:T(8,128)} %trial_ref.1, f32[1,8]{1,0:T(1,128)} %bitcast.5, f32[1,256]{1,0:T(1,128)} %bitcast.4, bf16[64,64,64]{2,1,0:T(8,128)(2,1)} %occ_hbm.1, bf16[64,256,512]{2,1,0:T(8,128)(2,1)} %virt_hbm.1, ...), custom_call_target="tpu_custom_call" | custom-call | tf_op jit(solution)/shard_map/pallas_call | solution.py:273
  59.4 1.5 %shard_map.87 = (f32[8,8,256]{2,1,0:T(8,128)}, f32[8,8]{1,0:T(8,128)}) custom-call(f32[8,8,256]{2,1,0:T(8,128)} %get-tuple-element.4.applied_ref, f32[8,8]{1,0:T(8,128)} %get-tuple-element.5.inter_ref), custom_call_target="tpu_custom_call" | custom-call | tf_op jit(solution)/shard_map/pallas_call | solution.py:289

commit v3 on v2

--- a/solution.py
+++ b/solution.py
@@ -10,6 +10,8 @@
 F32 = jnp.float32
 BF16 = jnp.bfloat16
 GROUPS = 1
+CHUNK = 16
+BLEND = 16
 MESH = pl.DeviceIdType.MESH
 
 
@@ -69,6 +71,15 @@
                 device_id=peer(da, dt), device_id_type=MESH))
         return copies
 
+    def contract(r, cols):
+        acc[...] = jnp.zeros_like(acc)
+
+        @pl.loop(0, slots // CHUNK)
+        def _(i):
+            acc[...] += jnp.dot(
+                blended[r, i], virt[pl.ds(i * CHUNK, CHUNK), :, cols].reshape(CHUNK * cond, cond),
+                preferred_element_type=F32)
+
     def apply(it, x):
         for r in range(groups):
             block = jnp.concatenate(x[r * size:(r + 1) * size], axis=1).astype(BF16)
@@ -114,17 +125,21 @@
                 copy.wait_recv()
             for s in range(naux):
                 wide[pl.ds(s * own_val, own_val), :] = block_recv[it, r, s].astype(F32)
-            rows = occ[...].reshape(slots * val, val)
-            for k in range(size):
-                column = wide[:, k * cond:(k + 1) * cond].astype(BF16)
-                b = jnp.dot(rows, column, preferred_element_type=F32).astype(BF16)
-                for q in range(slots):
-                    blended[r, k * val:(k + 1) * val, q * cond:(q + 1) * cond] = b[q * val:(q + 1) * val]
+            columns = [wide[:, k * cond:(k + 1) * cond].astype(BF16) for k in range(size)]
+
+            @pl.loop(0, slots // BLEND)
+            def _(i):
+                rows = occ[pl.ds(i * BLEND, BLEND)].reshape(BLEND * val, val)
+                for k in range(size):
+                    b = jnp.dot(rows, columns[k], preferred_element_type=F32).astype(BF16)
+                    for q in range(BLEND):
+                        blended[r, i * (BLEND // CHUNK) + q // CHUNK, k * val:(k + 1) * val,
+                                (q % CHUNK) * cond:(q % CHUNK + 1) * cond] = b[q * val:(q + 1) * val]
+
             if it == 0 and r == 0:
                 virt_copy.wait()
-            tr_send[it, r] = jnp.dot(
-                blended[r], virt[:, :, other_cols].reshape(slots * cond, cond),
-                preferred_element_type=F32).astype(BF16)
+            contract(r, other_cols)
+            tr_send[it, r] = acc[...].astype(BF16)
             copy = pltpu.make_async_remote_copy(
                 src_ref=tr_send.at[it, r], dst_ref=tr_recv.at[it, r],
                 send_sem=tr_ssem.at[it, r], recv_sem=tr_rsem.at[it, r],
@@ -134,9 +149,7 @@
 
         sums = []
         for r in range(groups):
-            acc[...] = jnp.dot(
-                blended[r], virt[:, :, own_cols].reshape(slots * cond, cond),
-                preferred_element_type=F32)
+            contract(r, own_cols)
             tr_copies[r].wait_recv()
             acc[...] += tr_recv[it, r].astype(F32)
             for s in range(naux):
@@ -244,7 +257,7 @@
         pltpu.VMEM(coef_occ.shape, BF16),
         pltpu.VMEM(coef_virt.shape, BF16),
         pltpu.VMEM(pair_coef.shape, BF16),
-        pltpu.VMEM((groups, size * val, slots * cond), BF16),
+        pltpu.VMEM((groups, slots // CHUNK, size * val, CHUNK * cond), BF16),
         pltpu.VMEM((size * val, cond), F32),
         pltpu.VMEM((val, size * cond), F32),
         pltpu.VMEM((own_val, half, cond), F32),

time: 61.1 us -> 57.8 us (0.946)
  Pallas kernels: 59.6 us -> 56.3 us
    pallas_call x1, Pallas kernels: 58.1 us -> 54.8 us  [body(): pl.pallas_call(functools.partial(kernel, naux, ntr, groups), out_shape=(j...]
where the time goes in v3:
time: 57.8 us; the launch traced here: 57.5 us
  Pallas kernels  56.3 us (97%)
  between operations  1.29 us (2%)
    pallas_call x1, Pallas kernels, body(): pl.pallas_call(functools.partial(kernel, naux, ntr, groups), out_shape=(j...  54.8 us
    pallas_call x1, Pallas kernels, body(): pl.pallas_call(finish, out_shape=(jax.ShapeDtypeStruct(trial_vectors.shap...  1.5 us

profile of v3, /device:TPU:0, one launch (start us, length us, event | category | flops | bytes accessed | tf_op | source)
XLA Modules:
  0.0 57.5 jit_solution(14018036475256556069)
XLA Ops:
  1.3 54.8 %shard_map.86 = (f32[8,8,256]{2,1,0:T(8,128)}, f32[8,8]{1,0:T(8,128)}) custom-call(s32[1,1]{1,0:T(1,128)} %bitcast.3.live_ref, f32[8,8,256]{2,1,0:T(8,128)} %trial_ref.1, f32[1,8]{1,0:T(1,128)} %bitcast.5, f32[1,256]{1,0:T(1,128)} %bitcast.4, bf16[64,64,64]{2,1,0:T(8,128)(2,1)} %occ_hbm.1, bf16[64,256,512]{2,1,0:T(8,128)(2,1)} %virt_hbm.1, ...), custom_call_target="tpu_custom_call" | custom-call | tf_op jit(solution)/shard_map/pallas_call | solution.py:286
  56.0 1.5 %shard_map.87 = (f32[8,8,256]{2,1,0:T(8,128)}, f32[8,8]{1,0:T(8,128)}) custom-call(f32[8,8,256]{2,1,0:T(8,128)} %get-tuple-element.4.applied_ref, f32[8,8]{1,0:T(8,128)} %get-tuple-element.5.inter_ref), custom_call_target="tpu_custom_call" | custom-call | tf_op jit(solution)/shard_map/pallas_call | solution.py:302

commit v4 on v3

--- a/solution.py
+++ b/solution.py
@@ -11,7 +11,7 @@
 BF16 = jnp.bfloat16
 GROUPS = 1
 CHUNK = 16
-BLEND = 16
+BLEND = 32
 MESH = pl.DeviceIdType.MESH
 
 
@@ -105,7 +105,7 @@
         proj = jnp.zeros((half, pair.shape[2]), F32)
         for v in range(own_val):
             proj += jnp.dot(mixed[v].astype(BF16), pair[v], preferred_element_type=F32)
-        proj_send[it] = proj
+        proj_send[it] = proj.astype(BF16)
         projections = to_all(it, proj_send, proj_recv, proj_ssem, proj_rsem)
         for copy in projections:
             copy.start()
@@ -138,18 +138,24 @@
 
             if it == 0 and r == 0:
                 virt_copy.wait()
-            contract(r, other_cols)
-            tr_send[it, r] = acc[...].astype(BF16)
             copy = pltpu.make_async_remote_copy(
                 src_ref=tr_send.at[it, r], dst_ref=tr_recv.at[it, r],
                 send_sem=tr_ssem.at[it, r], recv_sem=tr_rsem.at[it, r],
                 device_id=peer(0, 1), device_id_type=MESH)
-            copy.start()
             tr_copies.append(copy)
 
+            @pl.loop(0, 2)
+            def _(j):
+                start = pl.multiple_of(lax.rem(t + 1 + j, ntr) * cond, cond)
+                contract(r, pl.ds(start, cond))
+
+                @pl.when(j == 0)
+                def _():
+                    tr_send[it, r] = acc[...].astype(BF16)
+                    copy.start()
+
         sums = []
         for r in range(groups):
-            contract(r, own_cols)
             tr_copies[r].wait_recv()
             acc[...] += tr_recv[it, r].astype(F32)
             for s in range(naux):
@@ -166,9 +172,9 @@
 
         for copy in projections:
             copy.wait_recv()
-        proj = proj_send[it]
+        proj = proj_send[it].astype(F32)
         for da, dt in everyone:
-            proj += proj_recv[it, da * ntr + dt]
+            proj += proj_recv[it, da * ntr + dt].astype(F32)
         proj_b = proj.astype(BF16)
         for v in range(own_val):
             mixed[v] = lax.dot_general(
@@ -264,8 +270,8 @@
         pltpu.VMEM((vectors, own_val, cond), F32),
         pltpu.VMEM((2, groups, own_val, size * cond), BF16),
         pltpu.VMEM((2, groups, naux, own_val, size * cond), BF16),
-        pltpu.VMEM((2, half, naux_all), F32),
-        pltpu.VMEM((2, peers, half, naux_all), F32),
+        pltpu.VMEM((2, half, naux_all), BF16),
+        pltpu.VMEM((2, peers, half, naux_all), BF16),
         pltpu.VMEM((2, groups, size * val, cond), BF16),
         pltpu.VMEM((2, groups, size * val, cond), BF16),
         pltpu.VMEM((2, groups, naux, own_val, size * cond), BF16),

time: 57.8 us -> 57.2 us (0.990)
  Pallas kernels: 56.3 us -> 55.7 us
where the time goes in v4:
time: 57.2 us; the launch traced here: 57 us
  Pallas kernels  55.7 us (97%)
  between operations  1.29 us (2%)
    pallas_call x1, Pallas kernels, body(): pl.pallas_call(functools.partial(kernel, naux, ntr, groups), out_shape=(j...  54.2 us
    pallas_call x1, Pallas kernels, body(): pl.pallas_call(finish, out_shape=(jax.ShapeDtypeStruct(trial_vectors.shap...  1.5 us

profile of v4, /device:TPU:0, one launch (start us, length us, event | category | flops | bytes accessed | tf_op | source)
XLA Modules:
  0.0 57.0 jit_solution(16901541578776933460)
XLA Ops:
  1.3 54.2 %shard_map.86 = (f32[8,8,256]{2,1,0:T(8,128)}, f32[8,8]{1,0:T(8,128)}) custom-call(s32[1,1]{1,0:T(1,128)} %bitcast.3.live_ref, f32[8,8,256]{2,1,0:T(8,128)} %trial_ref.1, f32[1,8]{1,0:T(1,128)} %bitcast.5, f32[1,256]{1,0:T(1,128)} %bitcast.4, bf16[64,64,64]{2,1,0:T(8,128)(2,1)} %occ_hbm.1, bf16[64,256,512]{2,1,0:T(8,128)(2,1)} %virt_hbm.1, ...), custom_call_target="tpu_custom_call" | custom-call | tf_op jit(solution)/shard_map/pallas_call | solution.py:292
  55.5 1.5 %shard_map.87 = (f32[8,8,256]{2,1,0:T(8,128)}, f32[8,8]{1,0:T(8,128)}) custom-call(f32[8,8,256]{2,1,0:T(8,128)} %get-tuple-element.4.applied_ref, f32[8,8]{1,0:T(8,128)} %get-tuple-element.5.inter_ref), custom_call_target="tpu_custom_call" | custom-call | tf_op jit(solution)/shard_map/pallas_call | solution.py:308

commit v5 on v4

--- a/solution.py
+++ b/solution.py
@@ -10,7 +10,7 @@
 F32 = jnp.float32
 BF16 = jnp.bfloat16
 GROUPS = 1
-CHUNK = 16
+CHUNK = 32
 BLEND = 32
 MESH = pl.DeviceIdType.MESH
 

time: 57.2 us -> 56.6 us (0.990)
  Pallas kernels: 55.7 us -> 55.1 us
    pallas_call x1, Pallas kernels: 54.2 us -> 53.6 us  [body(): pl.pallas_call(functools.partial(kernel, naux, ntr, groups), out_shape=(j...]
where the time goes in v5:
time: 56.6 us; the launch traced here: 56.4 us
  Pallas kernels  55.1 us (97%)
  between operations  1.29 us (2%)
    pallas_call x1, Pallas kernels, body(): pl.pallas_call(functools.partial(kernel, naux, ntr, groups), out_shape=(j...  53.6 us
    pallas_call x1, Pallas kernels, body(): pl.pallas_call(finish, out_shape=(jax.ShapeDtypeStruct(trial_vectors.shap...  1.5 us

profile of v5, /device:TPU:0, one launch (start us, length us, event | category | flops | bytes accessed | tf_op | source)
XLA Modules:
  0.0 56.4 jit_solution(16120445365525724211)
XLA Ops:
  1.3 53.6 %shard_map.86 = (f32[8,8,256]{2,1,0:T(8,128)}, f32[8,8]{1,0:T(8,128)}) custom-call(s32[1,1]{1,0:T(1,128)} %bitcast.3.live_ref, f32[8,8,256]{2,1,0:T(8,128)} %trial_ref.1, f32[1,8]{1,0:T(1,128)} %bitcast.5, f32[1,256]{1,0:T(1,128)} %bitcast.4, bf16[64,64,64]{2,1,0:T(8,128)(2,1)} %occ_hbm.1, bf16[64,256,512]{2,1,0:T(8,128)(2,1)} %virt_hbm.1, ...), custom_call_target="tpu_custom_call" | custom-call | tf_op jit(solution)/shard_map/pallas_call | solution.py:292
  54.9 1.5 %shard_map.87 = (f32[8,8,256]{2,1,0:T(8,128)}, f32[8,8]{1,0:T(8,128)}) custom-call(f32[8,8,256]{2,1,0:T(8,128)} %get-tuple-element.4.applied_ref, f32[8,8]{1,0:T(8,128)} %get-tuple-element.5.inter_ref), custom_call_target="tpu_custom_call" | custom-call | tf_op jit(solution)/shard_map/pallas_call | solution.py:308
